TPU v7x, 512 devices: a whole 4x4x16 slice. The times are simulated.
512 devices in a mesh: dp: 128 (over z_lo, x, y, core), section: 4 (over z_hi).
Axes of the slice: x: 4, y: 4, z: 16 (z_hi: 4, z_lo: 4; z = z_hi * 4 + z_lo), core: 2. Of those that a mesh axis runs over, the one named last changes fastest.
Arguments:
- saved_inputs: bfloat16 [4, 2, 768, 6144], P('section', None, 'dp'), may hold values from -6 to 6
- carried: bfloat16 [4, 768, 6144], P('section', 'dp'), may hold values from -6 to 6
- head_grad: bfloat16 [768, 6144], P('dp'), may hold values from -6 to 6
- routing: int32 [4, 2, 768, 2], P('section', None, 'dp'), may hold values from 0 to 7, as said below
- replica_counts: int32 [128], replicated, may hold values from 2 to 5
- router: float32 [4, 6144, 8], P('section'), may hold values from -0.21875 to 0.21875
- w_in: bfloat16 [4, 128, 1536, 256], P('section', 'dp'), may hold values from -0.078125 to 0.078125
- w_out: bfloat16 [4, 128, 256, 1536], P('section', 'dp'), may hold values from -0.0625 to 0.0625
Outputs:
- input_grad: bfloat16 [2, 4, 768, 6144], P(None, 'section', 'dp')
- grad_in: bfloat16 [4, 128, 1536, 256], P('section', 'dp')
- grad_out: bfloat16 [4, 128, 256, 1536], P('section', 'dp')
- grad_router: float32 [4, 6144, 8], P('section')
Inputs may be any that keep to these rules, and one draw needn't show every extreme that they name: `routing`: each row names 2 different experts; in every section and step at most 2 of one device's 6 tokens name expert 0, and exactly 2 on some device.
All inputs are finite; a program needn't handle non-finite values.
Results may differ from a plain program's by a relative error of at most 0.0057.
Values may be sent and summed in bfloat16 or wider, within the bound.
A program may use at most 64 MiB of HBM per device.

v0:
```python
import jax
import jax.numpy as jnp
from jax import lax
from jax.sharding import PartitionSpec as P

STEPS = 2
CAP = 2


def shifted(array, axis, by):
    devices = lax.axis_size(axis)
    pairs = [(i, i + by) for i in range(devices) if 0 <= i + by < devices]
    return lax.ppermute(array, axis, pairs)


def from_partner(block, axis, distance):
    count = lax.axis_size(axis)
    route = []
    for low in range(count):
        high = low | 1 << distance
        if high != low and high < count:
            route += [(low, high), (high, low)]
    return lax.ppermute(block, axis, route)


def silu_grad(value):
    sig = jax.nn.sigmoid(value)
    return sig * (1.0 + value * (1.0 - sig))


def local(saved_inputs, carried, head_grad, routing, replica_counts, router, w_in, w_out):
    hi = lax.Precision.HIGHEST
    section_count = lax.axis_size("section")
    section_index = lax.axis_index("section")
    dev_count = lax.axis_size("dp")
    dev_index = lax.axis_index("dp")
    groups = dev_count // 4
    width = head_grad.shape[1]
    part = w_in.shape[2]
    hidden = w_in.shape[3]
    experts = router.shape[2]
    rows = dev_count * CAP
    weight_in = w_in[0, 0]
    weight_out = w_out[0, 0]
    router_w = router[0]
    quarter = dev_index % 4
    my_count = replica_counts[dev_index]
    first = (jnp.arange(experts) == 0).astype(jnp.float32)
    slots = jnp.arange(CAP, dtype=jnp.int32)

    def prepare(step):
        xin = saved_inputs[0, step]
        ids = routing[0, step]
        live = step + section_index < my_count
        xf = xin.astype(jnp.float32)
        logits = jnp.dot(xf, router_w, precision=hi)
        expo = jnp.exp(logits)
        prob = expo / jnp.sum(expo, axis=1, keepdims=True)
        routed = ((ids[:, 0] == 0) | (ids[:, 1] == 0)) & live
        flags = routed.astype(jnp.int32)
        slot = jnp.cumsum(flags, dtype=jnp.int32) - 1
        table = ((slot[None, :] == slots[:, None]) & routed[None, :]).astype(jnp.float32)
        xs = jnp.dot(table.astype(jnp.bfloat16), xin, preferred_element_type=jnp.float32).astype(
            jnp.bfloat16
        )
        gate = jnp.dot(table, prob[:, 0], precision=hi).astype(jnp.bfloat16)
        xsend = jnp.broadcast_to(
            xs.reshape(CAP, 4, part).transpose(1, 0, 2)[None], (groups, 4, CAP, part)
        ).reshape(dev_count, CAP, part)
        gsend = jnp.broadcast_to(gate[None], (dev_count, CAP))
        return (xf, prob, table, live, xsend, gsend)

    prepared = [prepare(step) for step in range(STEPS)]
    acc_in = jnp.zeros((part, hidden), jnp.float32)
    acc_out = jnp.zeros((hidden, part), jnp.float32)
    acc_router = jnp.zeros((width, experts), jnp.float32)
    outputs = []
    incoming = carried[0]
    for step in range(STEPS):
        xf, prob, table, live, xsend, gsend = prepared[step]
        if step == 1:
            passed = shifted(outputs[0], "section", -1)
            incoming = jnp.where(section_index == section_count - 1, head_grad, passed)
        grad_in_tok = jnp.where(live, incoming, jnp.zeros_like(incoming))
        ys = jnp.dot(
            table.astype(jnp.bfloat16), grad_in_tok, preferred_element_type=jnp.float32
        ).astype(jnp.bfloat16)
        ysend = jnp.broadcast_to(
            ys.reshape(CAP, 4, part).transpose(1, 0, 2)[None], (groups, 4, CAP, part)
        ).reshape(dev_count, CAP, part)
        recv_x, recv_y, recv_g = (
            lax.all_to_all(xsend, "dp", split_axis=0, concat_axis=0, tiled=True),
            lax.all_to_all(ysend, "dp", split_axis=0, concat_axis=0, tiled=True),
            lax.all_to_all(gsend, "dp", split_axis=0, concat_axis=0, tiled=True),
        )
        rows_x = recv_x.reshape(rows, part)
        rows_y = recv_y.reshape(rows, part)
        gate_f = recv_g.reshape(rows).astype(jnp.float32)[:, None]
        pre = jnp.dot(rows_x, weight_in, preferred_element_type=jnp.float32)
        upper = lax.dot_general(
            rows_y, weight_out, (((1,), (1,)), ((), ())), preferred_element_type=jnp.float32
        )
        for bit in range(2):
            other_pre, other_upper = from_partner((pre, upper), "dp", bit)
            pre = pre + other_pre
            upper = upper + other_upper
        act = jax.nn.silu(pre)
        dpre = (gate_f * upper * silu_grad(pre)).astype(jnp.bfloat16)
        scaled = (gate_f * act).astype(jnp.bfloat16)
        block_sum = jnp.sum(act * upper, axis=1)
        block_sum = jnp.where(quarter == 0, block_sum, jnp.zeros_like(block_sum)).astype(
            jnp.bfloat16
        )
        acc_in = acc_in + lax.dot_general(
            rows_x, dpre, (((0,), (0,)), ((), ())), preferred_element_type=jnp.float32
        )
        acc_out = acc_out + lax.dot_general(
            scaled, rows_y, (((0,), (0,)), ((), ())), preferred_element_type=jnp.float32
        )
        dx_part = lax.dot_general(
            dpre, weight_in, (((1,), (1,)), ((), ())), preferred_element_type=jnp.float32
        ).astype(jnp.bfloat16)
        back_x, back_g = (
            lax.all_to_all(
                dx_part.reshape(dev_count, CAP, part), "dp", split_axis=0, concat_axis=0, tiled=True
            ),
            lax.all_to_all(
                block_sum.reshape(dev_count, CAP), "dp", split_axis=0, concat_axis=0, tiled=True
            ),
        )
        summed = jnp.sum(back_x.astype(jnp.float32).reshape(groups, 4, CAP, part), axis=0)
        dxs = summed.transpose(1, 0, 2).reshape(CAP, width)
        dgate = jnp.sum(back_g.astype(jnp.float32), axis=0)
        dxe = lax.dot_general(table, dxs, (((0,), (0,)), ((), ())), precision=hi)
        dg_tok = lax.dot_general(table, dgate, (((0,), (0,)), ((), ())), precision=hi)
        dlog = (dg_tok * prob[:, 0])[:, None] * (first[None, :] - prob)
        result = grad_in_tok.astype(jnp.float32) + dxe + jnp.dot(dlog, router_w.T, precision=hi)
        outputs.append(result.astype(jnp.bfloat16))
        router_term = jnp.dot(xf.T, dlog, precision=hi)
        acc_router = acc_router + lax.psum(router_term, "dp")
    input_grad = jnp.stack(outputs)[:, None]
    grad_in = acc_in.astype(jnp.bfloat16)[None, None]
    grad_out = acc_out.astype(jnp.bfloat16)[None, None]
    return (input_grad, grad_in, grad_out, acc_router[None])


def solution(mesh):
    in_specs = (
        P("section", None, "dp", None),
        P("section", "dp", None),
        P("dp", None),
        P("section", None, "dp", None),
        P(),
        P("section", None, None),
        P("section", "dp", None, None),
        P("section", "dp", None, None),
    )
    out_specs = (
        P(None, "section", "dp", None),
        P("section", "dp", None, None),
        P("section", "dp", None, None),
        P("section", None, None),
    )
    return jax.shard_map(local, mesh=mesh, in_specs=in_specs, out_specs=out_specs, check_vma=False)
```

profile of v0, /device:TPU:128, one launch (start us, length us, event | category | flops | bytes accessed | tf_op | source)
XLA Modules:
  0.0 1498.4 jit_solution(10897805153019167695)
XLA Ops:
  10.7 1.9 fusion.54
  14.2 13.2 all-to-all-start.2
  27.6 23.9 %all-to-all-done.2 = bf16[128,2,1536]{2,1,0:T(2,128)(2,1)S(1)} async-done(((bf16[128,2,1536]{2,1,0:T(2,128)(2,1)}), bf16[128,2,1536]{2,1,0:T(2,128)(2,1)S(1)}, u32[]{:S(2)}, u32[]{:S(2)}) %all-to-all-start.2) | async-done | bytes 786464 | tf_op jit(solution)/shard_map/all_to_all | solution.py:92
  52.9 7.2 all-to-all-start.1
  64.0 20.0 %all-to-all-done.1 = bf16[128,2,1536]{2,1,0:T(2,128)(2,1)} async-done(((bf16[128,2,1536]{2,1,0:T(2,128)(2,1)}), bf16[128,2,1536]{2,1,0:T(2,128)(2,1)}, u32[]{:S(2)}, u32[]{:S(2)}) %all-to-all-start.1) | async-done | bytes 786464 | tf_op jit(solution)/shard_map/all_to_all | solution.py:93
  83.9 2.3 reshape.242
  86.6 1.9 collective-permute-start
  91.8 3.9 collective-permute-start.1
  96.6 6.1 all-to-all-start
  102.7 9.8 all-to-all-done
  117.1 6.6 all-to-all-start.4
  126.2 7.3 all-to-all-done.4
  133.5 6.2 all-to-all-start.3
  149.4 14.5 all-to-all-done.3
  163.9 2.0 broadcast_in_dim.25
  165.9 6.2 all-to-all-start.7
  179.7 9.9 collective-permute-done.4
  190.7 12.4 all-to-all-done.7
  204.5 11.7 all-to-all-start.6
  217.5 2.3 reshape.255
  222.9 17.1 %all-to-all-done.6 = bf16[128,2,1536]{2,1,0:T(2,128)(2,1)} async-done(((bf16[128,2,1536]{2,1,0:T(2,128)(2,1)}), bf16[128,2,1536]{2,1,0:T(2,128)(2,1)}, u32[]{:S(2)}, u32[]{:S(2)}) %all-to-all-start.6) | async-done | bytes 786464 | tf_op jit(solution)/shard_map/all_to_all | solution.py:93
  240.0 3.0 reshape.252
  251.3 3.9 collective-permute-start.6
  255.4 15.5 %all_to_all.54 = bf16[128,1,2]{2,1,0:T(2,128)(2,1)S(1)} all-to-all(bf16[128,1,2]{2,1,0:T(2,128)(2,1)S(1)} %broadcast_in_dim.23), channel_id=1, replica_groups=mesh['dp'=128,'section'=4] {'dp'}, dimensions={0} | all-to-all | bytes 1024 | tf_op jit(solution)/shard_map/all_to_all | solution.py:94
  271.8 2.0 multiply_reduce_fusion
  274.6 6.1 all-to-all-start.9
  280.7 2.2 convolution_convert_fusion.4
  282.9 2.8 reshape.256
  285.7 4.9 all-to-all-done.9
  290.6 7.5 all-to-all-start.8
  306.1 15.8 %all-to-all-done.8 = bf16[128,2,1536]{2,1,0:T(2,128)(2,1)} async-done(((bf16[128,2,1536]{2,1,0:T(2,128)(2,1)}), bf16[128,2,1536]{2,1,0:T(2,128)(2,1)}, u32[]{:S(2)}, u32[]{:S(2)}) %all-to-all-start.8) | async-done | bytes 786464 | tf_op jit(solution)/shard_map/all_to_all | solution.py:124
  327.1 1162.6 %all-reduce.2.cloned.1.call-done = f32[6144,8]{0,1:T(8,128)} async-done(((f32[6144,8]{0,1:T(8,128)}), f32[6144,8]{0,1:T(8,128)}) %all-reduce.2.cloned.1.call-update) | async-done | bytes 196624 | tf_op jit(solution)/shard_map/psum | solution.py:140
  (149 shorter events, 69.0 us)
Async XLA Ops:
  7.2 53.7 %copy-start = (bf16[1,1,1536,256]{3,2,1,0:T(8,128)(2,1)S(1)}, bf16[1,1,1536,256]{3,2,1,0:T(8,128)(2,1)}, u32[]{:S(2)}) copy-start(bf16[1,1,1536,256]{3,2,1,0:T(8,128)(2,1)} %param.14) | copy-start | bytes 2359300
  10.7 16.7 %copy-start.12 = (bf16[1,6,6144]{2,1,0:T(8,128)(2,1)S(1)}, bf16[1,6,6144]{2,1,0:T(8,128)(2,1)}, u32[]{:S(2)}) copy-start(bf16[1,6,6144]{2,1,0:T(8,128)(2,1)} %param.9) | copy-start | bytes 221188
  12.7 83.1 %copy-start.21 = (pred[2,6]{1,0:T(4,128)(4,1)}, pred[2,6]{1,0:T(4,128)(4,1)S(1)}, u32[]{:S(2)}) copy-start(pred[2,6]{1,0:T(4,128)(4,1)S(1)} %compare_and_fusion.1) | copy-start | bytes 40
  14.2 37.4 %all-to-all-start.2 = ((bf16[128,2,1536]{2,1,0:T(2,128)(2,1)}), bf16[128,2,1536]{2,1,0:T(2,128)(2,1)S(1)}, u32[]{:S(2)}, u32[]{:S(2)}) async-start(bf16[128,2,1536]{2,1,0:T(2,128)(2,1)} %bitcast.12), calls=%async_computation.2 | async-start | bytes 1572864 | tf_op jit(solution)/shard_map/all_to_all | solution.py:92
  27.4 32.7 %copy-start.4 = (f32[1,6144,8]{1,2,0:T(8,128)S(1)}, f32[1,6144,8]{1,2,0:T(8,128)}, u32[]{:S(2)}) copy-start(f32[1,6144,8]{1,2,0:T(8,128)} %param.13) | copy-start | bytes 589828
  52.9 31.1 %all-to-all-start.1 = ((bf16[128,2,1536]{2,1,0:T(2,128)(2,1)}), bf16[128,2,1536]{2,1,0:T(2,128)(2,1)}, u32[]{:S(2)}, u32[]{:S(2)}) async-start(bf16[128,2,1536]{2,1,0:T(2,128)(2,1)} %bitcast.9), calls=%async_computation.1 | async-start | bytes 1572864 | tf_op jit(solution)/shard_map/all_to_all | solution.py:93
  60.9 25.3 %copy-start.1 = (bf16[1,1,256,1536]{3,2,1,0:T(8,128)(2,1)S(1)}, bf16[1,1,256,1536]{3,2,1,0:T(8,128)(2,1)}, u32[]{:S(2)}) copy-start(bf16[1,1,256,1536]{3,2,1,0:T(8,128)(2,1)} %param.15) | copy-start | bytes 2359300
  62.0 26.7 %collective-permute-start.2 = (f32[256,256]{0,1:T(8,128)}, f32[256,256]{0,1:T(8,128)}, u32[]{:S(2)}, u32[]{:S(2)}) collective-permute-start(f32[256,256]{0,1:T(8,128)} %fusion.14), channel_id=1, source_target_pairs={{0,4},{4,0},{8,12},{12,8},{16,20},{20,16},{24,28},{28,24},{32,36},... | collective-permute-start | bytes 786440 | tf_op jit(solution)/shard_map/ppermute | solution.py:23
  86.6 5.1 collective-permute-start
  88.7 7.2 copy-start.26
  89.8 33.9 %copy-start.5 = (f32[256,256]{0,1:T(8,128)}, f32[256,256]{0,1:T(8,128)S(1)}, u32[]{:S(2)}) copy-start(f32[256,256]{0,1:T(8,128)S(1)} %add.89) | copy-start | bytes 786436
  89.8 24.5 %collective-permute-start.3 = (f32[256,256]{0,1:T(8,128)S(1)}, f32[256,256]{0,1:T(8,128)S(1)}, u32[]{:S(2)}, u32[]{:S(2)}) collective-permute-start(f32[256,256]{0,1:T(8,128)S(1)} %add.89), channel_id=1, source_target_pairs={{0,8},{8,0},{4,12},{12,4},{16,24},{24,16},{20,28},{28,20},{32,40},... | collective-permute-start | bytes 786440 | tf_op jit(solution)/shard_map/ppermute | solution.py:23
  91.8 22.6 %collective-permute-start.1 = (f32[256,256]{0,1:T(8,128)S(1)}, f32[256,256]{0,1:T(8,128)}, u32[]{:S(2)}, u32[]{:S(2)}) collective-permute-start(f32[256,256]{0,1:T(8,128)S(1)} %add.87), channel_id=1, source_target_pairs={{0,8},{8,0},{4,12},{12,4},{16,24},{24,16},{20,28},{28,20},{32,40},... | collective-permute-start | bytes 786440 | tf_op jit(solution)/shard_map/ppermute | solution.py:23
  96.6 16.0 %all-to-all-start = ((bf16[128,1,2]{2,1,0:T(2,128)(2,1)}), bf16[128,1,2]{2,1,0:T(2,128)(2,1)S(1)}, u32[]{:S(2)}, u32[]{:S(2)}) async-start(bf16[128,1,2]{2,1,0:T(2,128)(2,1)} %broadcast_in_dim.20), calls=%async_computation | async-start | bytes 131072 | tf_op jit(solution)/shard_map/all_to_all | solution.py:94
  114.4 9.3 copy-start.10
  117.1 16.5 %all-to-all-start.4 = ((bf16[128,1,2]{2,1,0:T(2,128)(2,1)}), bf16[128,1,2]{2,1,0:T(2,128)(2,1)S(1)}, u32[]{:S(2)}, u32[]{:S(2)}) async-start(bf16[128,1,2]{2,1,0:T(2,128)(2,1)} %convert_element_type.182), calls=%async_computation.4 | async-start | bytes 131072 | tf_op jit(solution)/shard_map/all_to_all | solution.py:127
  133.5 30.4 %all-to-all-start.3 = ((bf16[128,2,1536]{2,1,0:T(2,128)(2,1)}), bf16[128,2,1536]{2,1,0:T(2,128)(2,1)S(1)}, u32[]{:S(2)}, u32[]{:S(2)}) async-start(bf16[128,2,1536]{2,1,0:T(2,128)(2,1)} %reshape.246), calls=%async_computation.3 | async-start | bytes 1572864 | tf_op jit(solution)/shard_map/all_to_all | solution.py:124
  165.9 37.3 %all-to-all-start.7 = ((bf16[128,2,1536]{2,1,0:T(2,128)(2,1)}), bf16[128,2,1536]{2,1,0:T(2,128)(2,1)S(1)}, u32[]{:S(2)}, u32[]{:S(2)}) async-start(bf16[128,2,1536]{2,1,0:T(2,128)(2,1)} %bitcast.137), calls=%async_computation.7 | async-start | bytes 1572864 | tf_op jit(solution)/shard_map/all_to_all | solution.py:92
  172.3 17.3 %copy-start.23 = (pred[2,6]{1,0:T(4,128)(4,1)S(1)}, pred[2,6]{1,0:T(4,128)(4,1)}, u32[]{:S(2)}) copy-start(pred[2,6]{1,0:T(4,128)(4,1)} %copy-done.22) | copy-start | bytes 40
  177.7 11.9 collective-permute-start.4
  203.2 13.0 copy-start.2
  204.5 35.5 %all-to-all-start.6 = ((bf16[128,2,1536]{2,1,0:T(2,128)(2,1)}), bf16[128,2,1536]{2,1,0:T(2,128)(2,1)}, u32[]{:S(2)}, u32[]{:S(2)}) async-start(bf16[128,2,1536]{2,1,0:T(2,128)(2,1)} %bitcast.138), calls=%async_computation.6 | async-start | bytes 1572864 | tf_op jit(solution)/shard_map/all_to_all | solution.py:93
  221.0 25.9 %collective-permute-start.7 = (f32[256,256]{0,1:T(8,128)}, f32[256,256]{0,1:T(8,128)}, u32[]{:S(2)}, u32[]{:S(2)}) collective-permute-start(f32[256,256]{0,1:T(8,128)} %fusion.11), channel_id=1, source_target_pairs={{0,4},{4,0},{8,12},{12,8},{16,20},{20,16},{24,28},{28,24},{32,36},... | collective-permute-start | bytes 786440 | tf_op jit(solution)/shard_map/ppermute | solution.py:23
  244.7 5.8 collective-permute-start.5
  246.7 24.2 %copy-start.15 = (f32[6,8]{1,0:T(8,128)}, f32[6,8]{1,0:T(8,128)S(1)}, u32[]{:S(2)}) copy-start(f32[6,8]{1,0:T(8,128)S(1)} %broadcast_divide_fusion) | copy-start | bytes 580
  246.8 8.6 copy-start.27
  248.6 23.2 %collective-permute-start.8 = (f32[256,256]{0,1:T(8,128)}, f32[256,256]{0,1:T(8,128)}, u32[]{:S(2)}, u32[]{:S(2)}) collective-permute-start(f32[256,256]{0,1:T(8,128)} %add.99), channel_id=1, source_target_pairs={{0,8},{8,0},{4,12},{12,4},{16,24},{24,16},{20,28},{28,20},{32,40},... | collective-permute-start | bytes 786440 | tf_op jit(solution)/shard_map/ppermute | solution.py:23
  251.3 20.5 %collective-permute-start.6 = (f32[256,256]{0,1:T(8,128)}, f32[256,256]{0,1:T(8,128)}, u32[]{:S(2)}, u32[]{:S(2)}) collective-permute-start(f32[256,256]{0,1:T(8,128)} %add.97), channel_id=1, source_target_pairs={{0,8},{8,0},{4,12},{12,4},{16,24},{24,16},{20,28},{28,20},{32,40},... | collective-permute-start | bytes 786440 | tf_op jit(solution)/shard_map/ppermute | solution.py:23
  274.6 16.0 %all-to-all-start.9 = ((bf16[128,1,2]{2,1,0:T(2,128)(2,1)}), bf16[128,1,2]{2,1,0:T(2,128)(2,1)S(1)}, u32[]{:S(2)}, u32[]{:S(2)}) async-start(bf16[128,1,2]{2,1,0:T(2,128)(2,1)} %convert_element_type.183), calls=%async_computation.9 | async-start | bytes 131072 | tf_op jit(solution)/shard_map/all_to_all | solution.py:127
  290.6 31.3 %all-to-all-start.8 = ((bf16[128,2,1536]{2,1,0:T(2,128)(2,1)}), bf16[128,2,1536]{2,1,0:T(2,128)(2,1)}, u32[]{:S(2)}, u32[]{:S(2)}) async-start(bf16[128,2,1536]{2,1,0:T(2,128)(2,1)} %reshape.256), calls=%async_computation.8 | async-start | bytes 1572864 | tf_op jit(solution)/shard_map/all_to_all | solution.py:124
  298.1 1191.6 %all-reduce.2.cloned.1.call-start = ((), (), s32[]{:S(2)}) async-start(), calls=%async_computation.10 | async-start | bytes 393216 | tf_op jit(solution)/shard_map/psum | solution.py:140
  304.7 19.3 %copy-start.13 = (bf16[6,6144]{1,0:T(8,128)(2,1)S(1)}, bf16[6,6144]{1,0:T(8,128)(2,1)}, u32[]{:S(2)}) copy-start(bf16[6,6144]{1,0:T(8,128)(2,1)} %param.10) | copy-start | bytes 221188
  (16 other events, 39.1 us)
Sparse Core Ops, SparseCore 0:
  306.2 1183.4 all-reduce.1
where the time goes:
time: 1510 us; the launch traced here: 1500 us
  waiting for transfers between devices  1300 us (86%)
  starting transfers between devices  92.4 us (6%)
  local copies, waits for them, and re-layouts  33 us (2%)
  matrix products  25.1 us (2%)
  other arithmetic  17.6 us (1%)
  between operations  16.3 us (1%)
  blocking collectives  15.5 us (1%)
    psum x1, waiting for transfers between devices, local(): acc_router = acc_router + lax.psum(router_term, 'dp')  1160 us
    all_to_all x2, waiting for transfers between devices, local(): lax.all_to_all(ysend, 'dp', split_axis=0, concat_axis=0, tiled=True)  37.1 us
    all_to_all x2, waiting for transfers between devices, local(): lax.all_to_all(xsend, 'dp', split_axis=0, concat_axis=0, tiled=True)  36.4 us
    all_to_all x2, waiting for transfers between devices, local(): lax.all_to_all(dx_part.reshape(dev_count, CAP, part), 'dp', split_axis=0,...  30.3 us
  transfers between devices with their start and end apart: 19, of which 11 were waited for; matrix products, arithmetic and copies ran while one was open for 4% of the time, Pallas kernels for 0%

commit v1 on v0

--- a/solution.py
+++ b/solution.py
@@ -137,7 +137,7 @@
         result = grad_in_tok.astype(jnp.float32) + dxe + jnp.dot(dlog, router_w.T, precision=hi)
         outputs.append(result.astype(jnp.bfloat16))
         router_term = jnp.dot(xf.T, dlog, precision=hi)
-        acc_router = acc_router + lax.psum(router_term, "dp")
+        acc_router = acc_router + jnp.sum(lax.all_gather(router_term, "dp"), axis=0)
     input_grad = jnp.stack(outputs)[:, None]
     grad_in = acc_in.astype(jnp.bfloat16)[None, None]
     grad_out = acc_out.astype(jnp.bfloat16)[None, None]

time: 1510 us -> 675 us (0.45)
  the two profiles are of different devices: /device:TPU:128 before, /device:TPU:1 now
where the time goes in v1:
time: 675 us; the launch traced here: 665 us
  waiting for transfers between devices  420 us (62%)
  starting transfers between devices  106 us (16%)
  blocking collectives  40.8 us (6%)
  other arithmetic  32.7 us (5%)
  local copies, waits for them, and re-layouts  24.9 us (4%)
  matrix products  23.7 us (4%)
  between operations  16.4 us (2%)
    all_gather x2, waiting for transfers between devices, local(): acc_router = acc_router + jnp.sum(lax.all_gather(router_term, 'dp'), axis=0)  275 us
    all_to_all x2, waiting for transfers between devices, local(): lax.all_to_all(dx_part.reshape(dev_count, CAP, part), 'dp', split_axis=0,...  41.8 us
    all_to_all x2, waiting for transfers between devices, local(): lax.all_to_all(ysend, 'dp', split_axis=0, concat_axis=0, tiled=True)  41.6 us
    all_to_all x2, starting transfers between devices, local(): lax.all_to_all(ysend, 'dp', split_axis=0, concat_axis=0, tiled=True)  37.3 us
    all_to_all x2, waiting for transfers between devices, local(): lax.all_to_all(xsend, 'dp', split_axis=0, concat_axis=0, tiled=True)  31.6 us
    ppermute x8, starting transfers between devices, from_partner(): return lax.ppermute(block, axis, route)  23.7 us
    all_to_all x1, blocking collectives, local(): lax.all_to_all(gsend, 'dp', split_axis=0, concat_axis=0, tiled=True)  22.3 us
    all_to_all x1, blocking collectives, local(): lax.all_to_all(block_sum.reshape(dev_count, CAP), 'dp', split_axis=0, con...  18.5 us
  transfers between devices with their start and end apart: 19, of which 11 were waited for; matrix products, arithmetic and copies ran while one was open for 9% of the time, Pallas kernels for 0%

profile of v1, /device:TPU:1, one launch (start us, length us, event | category | flops | bytes accessed | tf_op | source)
XLA Modules:
  0.0 665.0 jit_solution(13142066124567442609)
XLA Ops:
  13.2 13.8 %all-to-all-start.1 = ((bf16[128,2,1536]{2,1,0:T(2,128)(2,1)}), bf16[128,2,1536]{2,1,0:T(2,128)(2,1)S(1)}, u32[]{:S(2)}, u32[]{:S(2)}) async-start(bf16[128,2,1536]{2,1,0:T(2,128)(2,1)} %bitcast.9), calls=%async_computation.1 | async-start | bytes 1572864 | tf_op jit(solution)/shard_map/all_to_all | solution.py:93
  27.5 23.4 %all-to-all-done.1 = bf16[128,2,1536]{2,1,0:T(2,128)(2,1)S(1)} async-done(((bf16[128,2,1536]{2,1,0:T(2,128)(2,1)}), bf16[128,2,1536]{2,1,0:T(2,128)(2,1)S(1)}, u32[]{:S(2)}, u32[]{:S(2)}) %all-to-all-start.1) | async-done | bytes 786464 | tf_op jit(solution)/shard_map/all_to_all | solution.py:93
  52.2 7.5 %all-to-all-start.2 = ((bf16[128,2,1536]{2,1,0:T(2,128)(2,1)}), bf16[128,2,1536]{2,1,0:T(2,128)(2,1)}, u32[]{:S(2)}, u32[]{:S(2)}) async-start(bf16[128,2,1536]{2,1,0:T(2,128)(2,1)} %bitcast.12), calls=%async_computation.2 | async-start | bytes 1572864 | tf_op jit(solution)/shard_map/all_to_all | solution.py:92
  60.9 3.0 collective-permute-start
  63.9 19.5 %all-to-all-done.2 = bf16[128,2,1536]{2,1,0:T(2,128)(2,1)} async-done(((bf16[128,2,1536]{2,1,0:T(2,128)(2,1)}), bf16[128,2,1536]{2,1,0:T(2,128)(2,1)}, u32[]{:S(2)}, u32[]{:S(2)}) %all-to-all-start.2) | async-done | bytes 786464 | tf_op jit(solution)/shard_map/all_to_all | solution.py:92
  83.3 2.3 reshape.257
  86.1 3.1 collective-permute-start.2
  92.4 3.4 collective-permute-start.3
  96.6 5.7 all-to-all-start
  102.4 10.1 %all-to-all-done = bf16[128,1,2]{2,1,0:T(2,128)(2,1)S(1)} async-done(((bf16[128,1,2]{2,1,0:T(2,128)(2,1)}), bf16[128,1,2]{2,1,0:T(2,128)(2,1)S(1)}, u32[]{:S(2)}, u32[]{:S(2)}) %all-to-all-start) | async-done | bytes 544 | tf_op jit(solution)/shard_map/all_to_all | solution.py:94
  115.4 6.4 all-to-all-start.4
  121.9 10.0 %all-to-all-done.4 = bf16[128,1,2]{2,1,0:T(2,128)(2,1)S(1)} async-done(((bf16[128,1,2]{2,1,0:T(2,128)(2,1)}), bf16[128,1,2]{2,1,0:T(2,128)(2,1)S(1)}, u32[]{:S(2)}, u32[]{:S(2)}) %all-to-all-start.4) | async-done | bytes 544 | tf_op jit(solution)/shard_map/all_to_all | solution.py:127
  135.8 5.9 all-to-all-start.3
  142.9 22.8 %all-to-all-done.3 = bf16[128,2,1536]{2,1,0:T(2,128)(2,1)S(1)} async-done(((bf16[128,2,1536]{2,1,0:T(2,128)(2,1)}), bf16[128,2,1536]{2,1,0:T(2,128)(2,1)S(1)}, u32[]{:S(2)}, u32[]{:S(2)}) %all-to-all-start.3) | async-done | bytes 786464 | tf_op jit(solution)/shard_map/all_to_all | solution.py:124
  167.0 10.9 %all-to-all-start.7 = ((bf16[128,2,1536]{2,1,0:T(2,128)(2,1)}), bf16[128,2,1536]{2,1,0:T(2,128)(2,1)S(1)}, u32[]{:S(2)}, u32[]{:S(2)}) async-start(bf16[128,2,1536]{2,1,0:T(2,128)(2,1)} %bitcast.144), calls=%async_computation.7 | async-start | bytes 1572864 | tf_op jit(solution)/shard_map/all_to_all | solution.py:92
  183.2 10.4 %collective-permute-done.4 = bf16[6,6144]{1,0:T(8,128)(2,1)} collective-permute-done((bf16[6,6144]{1,0:T(8,128)(2,1)}, bf16[6,6144]{1,0:T(8,128)(2,1)}, u32[]{:S(2)}, u32[]{:S(2)}) %collective-permute-start.4) | collective-permute-done | bytes 73760 | tf_op jit(solution)/shard_map/ppermute | solution.py:13
  194.8 12.1 %all-to-all-done.7 = bf16[128,2,1536]{2,1,0:T(2,128)(2,1)S(1)} async-done(((bf16[128,2,1536]{2,1,0:T(2,128)(2,1)}), bf16[128,2,1536]{2,1,0:T(2,128)(2,1)S(1)}, u32[]{:S(2)}, u32[]{:S(2)}) %all-to-all-start.7) | async-done | bytes 786464 | tf_op jit(solution)/shard_map/all_to_all | solution.py:92
  208.2 23.5 %all-to-all-start.6 = ((bf16[128,2,1536]{2,1,0:T(2,128)(2,1)}), bf16[128,2,1536]{2,1,0:T(2,128)(2,1)}, u32[]{:S(2)}, u32[]{:S(2)}) async-start(bf16[128,2,1536]{2,1,0:T(2,128)(2,1)} %bitcast.145), calls=%async_computation.6 | async-start | bytes 1572864 | tf_op jit(solution)/shard_map/all_to_all | solution.py:93
  232.3 2.3 reshape.267
  235.8 2.9 collective-permute-start.7
  238.6 18.2 %all-to-all-done.6 = bf16[128,2,1536]{2,1,0:T(2,128)(2,1)} async-done(((bf16[128,2,1536]{2,1,0:T(2,128)(2,1)}), bf16[128,2,1536]{2,1,0:T(2,128)(2,1)}, u32[]{:S(2)}, u32[]{:S(2)}) %all-to-all-start.6) | async-done | bytes 786464 | tf_op jit(solution)/shard_map/all_to_all | solution.py:93
  256.9 3.0 reshape.264
  265.5 5.6 collective-permute-start.8
  274.0 22.3 %all_to_all.54 = bf16[128,1,2]{2,1,0:T(2,128)(2,1)S(1)} all-to-all(bf16[128,1,2]{2,1,0:T(2,128)(2,1)S(1)} %broadcast_in_dim.21), channel_id=1, replica_groups=mesh['dp'=128,'section'=4] {'dp'}, dimensions={0} | all-to-all | bytes 1024 | tf_op jit(solution)/shard_map/all_to_all | solution.py:94
  300.5 18.5 %all_to_all.55 = bf16[128,1,2]{2,1,0:T(2,128)(2,1)S(1)} all-to-all(bf16[128,1,2]{2,1,0:T(2,128)(2,1)S(1)} %convert_element_type.183), channel_id=1, replica_groups=mesh['dp'=128,'section'=4] {'dp'}, dimensions={0} | all-to-all | bytes 1024 | tf_op jit(solution)/shard_map/all_to_all | solution.py:127
  323.8 2.9 reshape.268
  326.8 7.1 %all-to-all-start.8 = ((bf16[128,2,1536]{2,1,0:T(2,128)(2,1)}), bf16[128,2,1536]{2,1,0:T(2,128)(2,1)}, u32[]{:S(2)}, u32[]{:S(2)}) async-start(bf16[128,2,1536]{2,1,0:T(2,128)(2,1)} %reshape.268), calls=%async_computation.8 | async-start | bytes 1572864 | tf_op jit(solution)/shard_map/all_to_all | solution.py:124
  339.9 19.0 %all-to-all-done.8 = bf16[128,2,1536]{2,1,0:T(2,128)(2,1)} async-done(((bf16[128,2,1536]{2,1,0:T(2,128)(2,1)}), bf16[128,2,1536]{2,1,0:T(2,128)(2,1)}, u32[]{:S(2)}, u32[]{:S(2)}) %all-to-all-start.8) | async-done | bytes 786464 | tf_op jit(solution)/shard_map/all_to_all | solution.py:124
  364.1 47.9 %all-gather.5.cloned.1.call-done = f32[786432,8]{0,1:T(8,128)} async-done(((f32[6144,8]{0,1:T(8,128)}), f32[786432,8]{0,1:T(8,128)}) %all-gather.5.cloned.1.call-update) | async-done | bytes 25165840 | tf_op jit(solution)/shard_map/all_gather | solution.py:140
  412.0 9.2 %reduce_sum.98 = f32[6144,8]{0,1:T(8,128)S(1)} reduce(f32[128,6144,8]{1,2,0:T(8,128)} %bitcast.141, f32[]{:T(128)} %constant.43.clone.1), dimensions={0}, to_apply=%region_10.11 | reduce | flops 6242304 | bytes 25362436 | tf_op jit(solution)/shard_map/reduce_sum | solution.py:140
  421.2 226.9 %all-gather.7.cloned.1.call-done = f32[786432,8]{0,1:T(8,128)} async-done(((f32[6144,8]{0,1:T(8,128)}), f32[786432,8]{0,1:T(8,128)}) %all-gather.7.cloned.1.call-update) | async-done | bytes 25165840 | tf_op jit(solution)/shard_map/all_gather | solution.py:140
  648.1 9.2 %reduce_sum.99 = f32[6144,8]{0,1:T(8,128)S(1)} reduce(f32[128,6144,8]{1,2,0:T(8,128)} %bitcast.142, f32[]{:T(128)} %constant.43.clone.1), dimensions={0}, to_apply=%region_11.12 | reduce | flops 6242304 | bytes 25362436 | tf_op jit(solution)/shard_map/reduce_sum | solution.py:140
  (157 shorter events, 59.9 us)
Async XLA Ops:
  7.2 78.5 %copy-start = (bf16[1,1,1536,256]{3,2,1,0:T(8,128)(2,1)S(1)}, bf16[1,1,1536,256]{3,2,1,0:T(8,128)(2,1)}, u32[]{:S(2)}) copy-start(bf16[1,1,1536,256]{3,2,1,0:T(8,128)(2,1)} %param.14) | copy-start | bytes 2359300
  10.8 85.0 %copy-start.25 = (pred[2,6]{1,0:T(4,128)(4,1)}, pred[2,6]{1,0:T(4,128)(4,1)S(1)}, u32[]{:S(2)}) copy-start(pred[2,6]{1,0:T(4,128)(4,1)S(1)} %compare_and_fusion.1) | copy-start | bytes 40
  13.2 37.7 %all-to-all-start.1 = ((bf16[128,2,1536]{2,1,0:T(2,128)(2,1)}), bf16[128,2,1536]{2,1,0:T(2,128)(2,1)S(1)}, u32[]{:S(2)}, u32[]{:S(2)}) async-start(bf16[128,2,1536]{2,1,0:T(2,128)(2,1)} %bitcast.9), calls=%async_computation.1 | async-start | bytes 1572864 | tf_op jit(solution)/shard_map/all_to_all | solution.py:93
  27.0 32.7 %copy-start.6 = (f32[1,6144,8]{1,2,0:T(8,128)S(1)}, f32[1,6144,8]{1,2,0:T(8,128)}, u32[]{:S(2)}) copy-start(f32[1,6144,8]{1,2,0:T(8,128)} %param.13) | copy-start | bytes 589828
  27.3 32.4 %copy-start.9 = (bf16[1,1,6,6144]{3,1,2,0:T(2,128)(2,1)}, bf16[1,1,6,6144]{3,1,2,0:T(2,128)(2,1)S(1)}, u32[]{:S(2)}) copy-start(bf16[1,1,6,6144]{3,1,2,0:T(2,128)(2,1)S(1)} %get-tuple-element.24) | copy-start | bytes 221188
  52.2 31.2 %all-to-all-start.2 = ((bf16[128,2,1536]{2,1,0:T(2,128)(2,1)}), bf16[128,2,1536]{2,1,0:T(2,128)(2,1)}, u32[]{:S(2)}, u32[]{:S(2)}) async-start(bf16[128,2,1536]{2,1,0:T(2,128)(2,1)} %bitcast.12), calls=%async_computation.2 | async-start | bytes 1572864 | tf_op jit(solution)/shard_map/all_to_all | solution.py:92
  60.9 28.5 %collective-permute-start = (f32[256,256]{0,1:T(8,128)S(1)}, f32[256,256]{0,1:T(8,128)}, u32[]{:S(2)}, u32[]{:S(2)}) collective-permute-start(f32[256,256]{0,1:T(8,128)S(1)} %fusion.17), channel_id=1, source_target_pairs={{0,4},{4,0},{8,12},{12,8},{16,20},{20,16},{24,28},{28,24},{32,36},... | collective-permute-start | bytes 786440 | tf_op jit(solution)/shard_map/ppermute | solution.py:23
  86.1 6.3 collective-permute-start.2
  89.3 42.9 %copy-start.15 = (f32[6,8]{1,0:T(8,128)}, f32[6,8]{1,0:T(8,128)S(1)}, u32[]{:S(2)}) copy-start(f32[6,8]{1,0:T(8,128)S(1)} %broadcast_divide_fusion.1) | copy-start | bytes 580
  89.4 42.8 %copy-start.10 = (bf16[1,1,6,6144]{3,1,2,0:T(2,128)(2,1)S(1)}, bf16[1,1,6,6144]{3,1,2,0:T(2,128)(2,1)}, u32[]{:S(2)}) copy-start(bf16[1,1,6,6144]{3,1,2,0:T(2,128)(2,1)} %copy-done.9) | copy-start | bytes 221188
  90.4 22.3 %collective-permute-start.1 = (f32[256,256]{0,1:T(8,128)S(1)}, f32[256,256]{0,1:T(8,128)}, u32[]{:S(2)}, u32[]{:S(2)}) collective-permute-start(f32[256,256]{0,1:T(8,128)S(1)} %add.93), channel_id=1, source_target_pairs={{0,8},{8,0},{4,12},{12,4},{16,24},{24,16},{20,28},{28,20},{32,40},... | collective-permute-start | bytes 786440 | tf_op jit(solution)/shard_map/ppermute | solution.py:23
  92.4 40.8 %copy-start.7 = (f32[256,256]{0,1:T(8,128)}, f32[256,256]{0,1:T(8,128)S(1)}, u32[]{:S(2)}) copy-start(f32[256,256]{0,1:T(8,128)S(1)} %add.95) | copy-start | bytes 786436
  92.4 20.4 %collective-permute-start.3 = (f32[256,256]{0,1:T(8,128)S(1)}, f32[256,256]{0,1:T(8,128)}, u32[]{:S(2)}, u32[]{:S(2)}) collective-permute-start(f32[256,256]{0,1:T(8,128)S(1)} %add.95), channel_id=1, source_target_pairs={{0,8},{8,0},{4,12},{12,4},{16,24},{24,16},{20,28},{28,20},{32,40},... | collective-permute-start | bytes 786440 | tf_op jit(solution)/shard_map/ppermute | solution.py:23
  95.9 36.1 %copy-start.26 = (pred[2,6]{1,0:T(4,128)(4,1)S(1)}, pred[2,6]{1,0:T(4,128)(4,1)}, u32[]{:S(2)}) copy-start(pred[2,6]{1,0:T(4,128)(4,1)} %copy-done.25) | copy-start | bytes 40
  96.6 15.8 %all-to-all-start = ((bf16[128,1,2]{2,1,0:T(2,128)(2,1)}), bf16[128,1,2]{2,1,0:T(2,128)(2,1)S(1)}, u32[]{:S(2)}, u32[]{:S(2)}) async-start(bf16[128,1,2]{2,1,0:T(2,128)(2,1)} %broadcast_in_dim.18), calls=%async_computation | async-start | bytes 131072 | tf_op jit(solution)/shard_map/all_to_all | solution.py:94
  115.4 16.5 %all-to-all-start.4 = ((bf16[128,1,2]{2,1,0:T(2,128)(2,1)}), bf16[128,1,2]{2,1,0:T(2,128)(2,1)S(1)}, u32[]{:S(2)}, u32[]{:S(2)}) async-start(bf16[128,1,2]{2,1,0:T(2,128)(2,1)} %convert_element_type.182), calls=%async_computation.4 | async-start | bytes 131072 | tf_op jit(solution)/shard_map/all_to_all | solution.py:127
  121.8 290.2 %all-gather.5.cloned.1.call-start = ((), (), s32[]{:S(2)}) async-start(), calls=%async_computation.10 | async-start | bytes 25362432 | tf_op jit(solution)/shard_map/all_gather | solution.py:140
  121.9 59.0 %copy-start.22 = (f32[8]{0:T(128)}, f32[8]{0:T(128)S(1)}, u32[]{:S(2)}) copy-start(f32[8]{0:T(128)S(1)} %compare_convert_fusion) | copy-start | bytes 100
  135.8 29.9 %all-to-all-start.3 = ((bf16[128,2,1536]{2,1,0:T(2,128)(2,1)}), bf16[128,2,1536]{2,1,0:T(2,128)(2,1)S(1)}, u32[]{:S(2)}, u32[]{:S(2)}) async-start(bf16[128,2,1536]{2,1,0:T(2,128)(2,1)} %reshape.258), calls=%async_computation.3 | async-start | bytes 1572864 | tf_op jit(solution)/shard_map/all_to_all | solution.py:124
  142.6 131.2 %copy-start.28 = (pred[2,6]{1,0:T(4,128)(4,1)}, pred[2,6]{1,0:T(4,128)(4,1)S(1)}, u32[]{:S(2)}) copy-start(pred[2,6]{1,0:T(4,128)(4,1)S(1)} %compare_and_fusion) | copy-start | bytes 40
  142.9 36.8 %copy-start.27 = (pred[2,6]{1,0:T(4,128)(4,1)S(1)}, pred[2,6]{1,0:T(4,128)(4,1)}, u32[]{:S(2)}) copy-start(pred[2,6]{1,0:T(4,128)(4,1)} %copy-done.25) | copy-start | bytes 40
  167.0 39.9 %all-to-all-start.7 = ((bf16[128,2,1536]{2,1,0:T(2,128)(2,1)}), bf16[128,2,1536]{2,1,0:T(2,128)(2,1)S(1)}, u32[]{:S(2)}, u32[]{:S(2)}) async-start(bf16[128,2,1536]{2,1,0:T(2,128)(2,1)} %bitcast.144), calls=%async_computation.7 | async-start | bytes 1572864 | tf_op jit(solution)/shard_map/all_to_all | solution.py:92
  181.9 11.7 %collective-permute-start.4 = (bf16[6,6144]{1,0:T(8,128)(2,1)}, bf16[6,6144]{1,0:T(8,128)(2,1)}, u32[]{:S(2)}, u32[]{:S(2)}) collective-permute-start(bf16[6,6144]{1,0:T(8,128)(2,1)} %fusion), channel_id=1, source_target_pairs={{1,0},{2,1},{3,2},{5,4},{6,5},{7,6},{9,8},{10,9},{11,10},{13,12},{... | collective-permute-start | bytes 221192 | tf_op jit(solution)/shard_map/ppermute | solution.py:13
  206.9 25.0 %copy-start.4 = (bf16[128,2,1536]{2,1,0:T(2,128)(2,1)}, bf16[128,2,1536]{2,1,0:T(2,128)(2,1)S(1)}, u32[]{:S(2)}) copy-start(bf16[128,2,1536]{2,1,0:T(2,128)(2,1)S(1)} %all-to-all-done.7) | copy-start | bytes 2359300
  208.2 48.7 %all-to-all-start.6 = ((bf16[128,2,1536]{2,1,0:T(2,128)(2,1)}), bf16[128,2,1536]{2,1,0:T(2,128)(2,1)}, u32[]{:S(2)}, u32[]{:S(2)}) async-start(bf16[128,2,1536]{2,1,0:T(2,128)(2,1)} %bitcast.145), calls=%async_computation.6 | async-start | bytes 1572864 | tf_op jit(solution)/shard_map/all_to_all | solution.py:93
  231.7 416.4 %all-gather.7.cloned.1.call-start = ((), (), s32[]{:S(2)}) async-start(), calls=%async_computation.11 | async-start | bytes 25362432 | tf_op jit(solution)/shard_map/all_gather | solution.py:140
  235.8 28.0 %collective-permute-start.7 = (f32[256,256]{0,1:T(8,128)}, f32[256,256]{0,1:T(8,128)}, u32[]{:S(2)}, u32[]{:S(2)}) collective-permute-start(f32[256,256]{0,1:T(8,128)} %fusion.10), channel_id=1, source_target_pairs={{0,4},{4,0},{8,12},{12,8},{16,20},{20,16},{24,28},{28,24},{32,36},... | collective-permute-start | bytes 786440 | tf_op jit(solution)/shard_map/ppermute | solution.py:23
  261.6 9.5 %collective-permute-start.5 = (f32[256,256]{0,1:T(8,128)S(1)}, f32[256,256]{0,1:T(8,128)S(1)}, u32[]{:S(2)}, u32[]{:S(2)}) collective-permute-start(f32[256,256]{0,1:T(8,128)S(1)} %fusion.15), channel_id=1, source_target_pairs={{0,4},{4,0},{8,12},{12,8},{16,20},{20,16},{24,28},{28,24},{32,36},... | collective-permute-start | bytes 786440 | tf_op jit(solution)/shard_map/ppermute | solution.py:23
  263.6 32.7 %copy-start.17 = (f32[6,8]{1,0:T(8,128)}, f32[6,8]{1,0:T(8,128)S(1)}, u32[]{:S(2)}) copy-start(f32[6,8]{1,0:T(8,128)S(1)} %broadcast_divide_fusion) | copy-start | bytes 580
  265.5 31.6 %collective-permute-start.8 = (f32[256,256]{0,1:T(8,128)}, f32[256,256]{0,1:T(8,128)}, u32[]{:S(2)}, u32[]{:S(2)}) collective-permute-start(f32[256,256]{0,1:T(8,128)} %add.105), channel_id=1, source_target_pairs={{0,8},{8,0},{4,12},{12,4},{16,24},{24,16},{20,28},{28,20},{32,40},... | collective-permute-start | bytes 786440 | tf_op jit(solution)/shard_map/ppermute | solution.py:23
  271.9 25.3 %collective-permute-start.6 = (f32[256,256]{0,1:T(8,128)}, f32[256,256]{0,1:T(8,128)}, u32[]{:S(2)}, u32[]{:S(2)}) collective-permute-start(f32[256,256]{0,1:T(8,128)} %add.103), channel_id=1, source_target_pairs={{0,8},{8,0},{4,12},{12,4},{16,24},{24,16},{20,28},{28,20},{32,40},... | collective-permute-start | bytes 786440 | tf_op jit(solution)/shard_map/ppermute | solution.py:23
  326.8 32.2 %all-to-all-start.8 = ((bf16[128,2,1536]{2,1,0:T(2,128)(2,1)}), bf16[128,2,1536]{2,1,0:T(2,128)(2,1)}, u32[]{:S(2)}, u32[]{:S(2)}) async-start(bf16[128,2,1536]{2,1,0:T(2,128)(2,1)} %reshape.268), calls=%async_computation.8 | async-start | bytes 1572864 | tf_op jit(solution)/shard_map/all_to_all | solution.py:124
  (18 other events, 207.6 us)
Sparse Core Ops, SparseCore 0:
  133.4 278.5 all-gather.4
  414.1 233.8 all-gather.6
